TPU v7x, 256 devices: a whole 4x4x8 slice. The times are simulated.
256 devices in a mesh: row: 16 (over z, core), col: 16 (over x, y).
Axes of the slice: x: 4, y: 4, z: 8, core: 2. Of those that a mesh axis runs over, the one named last changes fastest.
Arguments:
- child_samples: bfloat16 [2, 2, 256, 262144], P(None, None, 'col', 'row'), may hold values from -6 to 6
- child_map: int32 [2, 2048], P(None, 'row'), may hold values from 0 to 127, as said below
- forward_probe: bfloat16 [256, 262144], P(None, ('row', 'col')), may hold values from -6 to 6
- adjoint_probe: bfloat16 [256, 262144], P(None, ('row', 'col')), may hold values from -6 to 6
- stored_sparse_blocks: bfloat16 [2048, 18, 128, 128], P(('row', 'col')), may hold values from -0.125 to 0.125
- block_pattern: int32 [16, 128, 18], P(None, 'col'), may hold values from 0 to 7
Outputs:
- row_basis: bfloat16 [256, 262144], P(None, ('row', 'col'))
- column_basis: bfloat16 [256, 262144], P(None, ('row', 'col'))
- transfers: float32 [2, 2, 65536, 256], P(None, None, ('row', 'col'))
Inputs may be any that keep to these rules, and one draw needn't show every extreme that they name: Within each aligned group of 16 * 8 front blocks (one row group), each row of child_map is a permutation of 0 to 16 * 8 - 1.
All inputs are finite; a program needn't handle non-finite values.
Results may differ from a plain program's by a relative error of at most 0.0055.
Values may be sent and summed in bfloat16 or wider, within the bound.
A program may use at most 128 MiB of HBM per device.

v0:
```python
from functools import partial
import math
import jax
import jax.numpy as jnp
from jax import lax
from jax.sharding import PartitionSpec as P

S = 256
BLK = 128
SLOTS = 6


def padded(x, sides, width):
    for axis, dim in sides:
        peers, length = (lax.axis_size(axis), x.shape[dim])
        up = [(i, (i + 1) % peers) for i in range(peers - 1)]
        down = [(j, i) for i, j in up]
        last = lax.slice_in_dim(x, length - width, length, axis=dim)
        leading = lax.slice_in_dim(x, 0, width, axis=dim)
        before = lax.ppermute(last, axis, up)
        after = lax.ppermute(leading, axis, down)
        x = jnp.concatenate([before, x, after], axis=dim)
    return x


def shifted(block, axis, distance):
    devices = range(lax.axis_size(axis))
    route = [(i - distance, i) for i in devices if i - distance in devices]
    return lax.ppermute(block, axis, route)


def from_partner(value, axis, bit):
    mask = 2**bit
    pairs = [(source, source ^ mask) for source in range(lax.axis_size(axis))]
    return lax.ppermute(value, axis, pairs)


def spread_terms(targets, sketch_products, width):
    onehot = (targets[..., None] == jnp.arange(width, dtype=jnp.int32)).astype(jnp.float32)
    return jnp.einsum("bkg,bksc->sgc", onehot, sketch_products, precision=lax.Precision.HIGHEST)


def local(
    child_samples, child_map, forward_probe, adjoint_probe, stored_sparse_blocks, block_pattern
):
    samples_here = child_samples.shape[2]
    rows_group = child_samples.shape[3]
    group_blocks = rows_group // BLK
    leaf_rows = forward_probe.shape[1]
    leaf_blocks = leaf_rows // BLK
    row_pos = lax.axis_index("row")
    blocked = child_samples.reshape(2, 2, samples_here, group_blocks, BLK)
    first_child = jnp.take(blocked[0], child_map[0], axis=2).astype(jnp.float32)
    second_child = jnp.take(blocked[1], child_map[1], axis=2).astype(jnp.float32)
    extended = (
        (first_child + second_child).astype(jnp.bfloat16).reshape(2, samples_here, rows_group)
    )
    regrouped = lax.all_to_all(extended, "col", split_axis=2, concat_axis=1, tiled=True)
    own_pattern = lax.dynamic_index_in_dim(block_pattern, row_pos, 0, keepdims=False)
    regions = jnp.arange(3 * SLOTS, dtype=jnp.int32) // SLOTS
    flat_index = regions[None, :] * leaf_blocks + own_pattern
    probe_ext = padded(forward_probe, (("row", 1),), leaf_rows)
    conjugate_transpose_rows = adjoint_probe.reshape(S, leaf_blocks, BLK)
    sketch_products = jnp.einsum(
        "mda,duai->dumi",
        conjugate_transpose_rows,
        stored_sparse_blocks,
        preferred_element_type=jnp.float32,
    )
    terms = spread_terms(flat_index, sketch_products, 3 * leaf_blocks).reshape(S, 3, leaf_rows)
    from_above = shifted(terms[:, 0].astype(jnp.bfloat16), "row", -1).astype(jnp.float32)
    from_below = shifted(terms[:, 2].astype(jnp.bfloat16), "row", 1).astype(jnp.float32)
    adjoint_sparse = terms[:, 1] + from_above + from_below
    probe_blocks = probe_ext.reshape(S, 3 * leaf_blocks, BLK)
    selector = (flat_index[..., None] == jnp.arange(3 * leaf_blocks, dtype=jnp.int32)).astype(
        jnp.bfloat16
    )
    collected_samples = jnp.einsum(
        "jhc,wct->wjht", selector, probe_blocks, preferred_element_type=jnp.float32
    ).astype(jnp.bfloat16)
    forward_sparse = jnp.einsum(
        "wjht,jhot->wjo",
        collected_samples,
        stored_sparse_blocks,
        preferred_element_type=jnp.float32,
    ).reshape(S, leaf_rows)
    samples = jnp.stack(
        [
            regrouped[0].astype(jnp.float32) + forward_sparse,
            regrouped[1].astype(jnp.float32) + adjoint_sparse,
        ]
    )
    grams = jnp.einsum("ksr,ktr->kst", samples, samples, precision=lax.Precision.HIGHEST)
    level_one = grams + from_partner(grams.astype(jnp.bfloat16), "col", 0).astype(grams.dtype)
    level_two = level_one + from_partner(level_one.astype(jnp.bfloat16), "col", 1).astype(
        level_one.dtype
    )
    stacked_grams = jnp.concatenate([grams, level_one, level_two], axis=0)
    factors = jnp.linalg.cholesky(stacked_grams)
    identity = jnp.broadcast_to(jnp.eye(S, dtype=jnp.float32), factors.shape)
    inverses = jax.vmap(partial(jax.scipy.linalg.solve_triangular, lower=True))(factors, identity)
    factor_leaf = factors[0:2]
    factor_one = factors[2:4]
    inverse_leaf = inverses[0:2]
    inverse_one = inverses[2:4]
    inverse_two = inverses[4:6]
    bases = (
        jnp.einsum("kst,ktr->ksr", inverse_leaf, samples, precision=lax.Precision.HIGHEST)
        * math.sqrt(leaf_rows)
    ).astype(jnp.bfloat16)
    first = jnp.einsum("kst,ktu->kus", inverse_one, factor_leaf, precision=lax.Precision.HIGHEST)
    second = jnp.einsum("kst,ktu->kus", inverse_two, factor_one, precision=lax.Precision.HIGHEST)
    transfers = jnp.stack([first, second], axis=1)
    return (bases[0], bases[1], transfers)


def solution(mesh):
    return jax.shard_map(
        local,
        mesh=mesh,
        in_specs=(
            P(None, None, "col", "row"),
            P(None, "row"),
            P(None, ("row", "col")),
            P(None, ("row", "col")),
            P(("row", "col"), None, None, None),
            P(None, "col", None),
        ),
        out_specs=(
            P(None, ("row", "col")),
            P(None, ("row", "col")),
            P(None, None, ("row", "col"), None),
        ),
        check_vma=False,
    )
```

profile of v0, /device:TPU:98, one launch (start us, length us, event | category | flops | bytes accessed | tf_op | source)
XLA Modules:
  0.0 524.5 jit_solution(15192901601436697136)
XLA Ops:
  2.6 2.4 collective-permute-start
  12.9 12.7 %copy.136 = bf16[2,16,128,128]{1,0,3,2:T(2,128)(2,1)} copy(bf16[2,16,128,128]{3,1,0,2:T(8,128)(2,1)S(1)} %add_convert_fusion) | data formatting | bytes 2097152 | tf_op jit(solution)/shard_map/reshape | solution.py:56
  25.6 11.2 %reshape.174 = bf16[16,2,16384]{2,1,0:T(2,128)(2,1)} reshape(bf16[16384,2,16]{2,1,0:T(2,128)(2,1)} %bitcast.127) | data formatting | bytes 2097152
  36.9 7.6 %all-to-all-start = ((bf16[16,2,16384]{2,1,0:T(2,128)(2,1)}), bf16[16,2,16384]{2,1,0:T(2,128)(2,1)}, u32[]{:S(2)}, u32[]{:S(2)}) async-start(bf16[16,2,16384]{2,1,0:T(2,128)(2,1)} %reshape.174), calls=%async_computation | async-start | bytes 2097152 | tf_op jit(solution)/shard_map/all_to_all | solution.py:58
  44.6 11.5 %convolution_bitcast_fusion = f32[8,18,256,128]{2,3,1,0:T(8,128)} fusion(bf16[8,18,128,128]{3,2,1,0:T(8,128)(2,1)} %param.12, bf16[256,8,128,1]{2,1,0,3:T(8,128)(2,1)S(1)} %bitcast.136), kind=kOutput, calls=%fused_computation.7 | convolution fusion | flops 1207959552 | bytes 24117248 | tf_op jit(solution)/shard_map/mda,duai->dumi/dot_general | solution.py:64
  56.1 22.1 %copy.108 = f32[8,18,256,128]{3,1,0,2:T(8,128)} copy(f32[8,18,256,128]{2,3,1,0:T(8,128)} %convolution_bitcast_fusion) | data formatting | bytes 37748736 | tf_op jit(solution)/shard_map/mda,duai->dumi/transpose | solution.py:64
  78.9 12.8 %convolution_bitcast_fusion.1 = f32[256,24,128]{2,1,0:T(8,128)S(1)} fusion(f32[8,18,256,128]{3,1,0,2:T(8,128)} %copy.108, s32[8,18]{1,0:T(8,128)S(1)} %bitcast_add_fusion.2), kind=kOutput, calls=%fused_computation.11 | convolution fusion | flops 1358957952 | bytes 22020672 | tf_op jit(solution)/shard_map/bkg,bksc->sgc/dot_general | solution.py:40
  91.7 2.4 copy.109
  94.1 2.4 copy.110
  97.7 4.1 collective-permute-start.3
  106.2 6.4 %convert_bitcast_fusion = bf16[256,8,18,128]{3,2,1,0:T(8,128)(2,1)} fusion(bf16[256,24,128,1]{2,1,0,3:T(8,128)(2,1)S(1)} %bitcast.130, s32[8,18]{1,0:T(8,128)S(1)} %bitcast_add_fusion.2), kind=kOutput, calls=%fused_computation.4 | convolution fusion | flops 231214464 | bytes 11010624 | tf_op jit(solution)/shard_map/jhc,wct->wjht/dot_general | solution.py:78
  112.5 12.4 %fusion = f32[8,256,128,1]{1,2,3,0:T(8,128)} fusion(bf16[8,18,128,128]{3,2,1,0:T(8,128)(2,1)} %param.12, bf16[256,8,18,128]{3,2,1,0:T(8,128)(2,1)} %convert_bitcast_fusion), kind=kOutput, calls=%fused_computation.5 | convolution fusion | flops 1207959552 | bytes 15204352 | tf_op jit(solution)/shard_map/wjht,jhot->wjo/dot_general | solution.py:81
  125.0 2.6 copy.104
  127.6 8.9 %reshape.175 = bf16[16384,2,16]{2,1,0:T(2,128)(2,1)} reshape(bf16[16,2,16384]{2,1,0:T(2,128)(2,1)} %all-to-all-done) | data formatting | bytes 2097152
  136.5 12.7 %copy.137 = bf16[2,16,16,1024]{3,2,1,0:T(8,128)(2,1)} copy(bf16[2,16,16,1024]{1,0,3,2:T(2,128)(2,1)} %bitcast.128) | data formatting | bytes 2097152 | tf_op jit(solution)/shard_map/all_to_all | solution.py:58
  154.5 2.3 fusion.57
  159.0 6.9 %collective-permute-done.4 = bf16[2,256,256]{1,2,0:T(8,128)(2,1)S(1)} collective-permute-done((bf16[2,256,256]{1,2,0:T(8,128)(2,1)S(1)}, bf16[2,256,256]{1,2,0:T(8,128)(2,1)S(1)}, u32[]{:S(2)}, u32[]{:S(2)}) %collective-permute-start.4) | collective-permute-done | bytes 262176 | tf_op jit(solution)/shard_map/ppermute | solution.py:35
  166.0 3.0 collective-permute-start.5
  170.4 5.6 %collective-permute-done.5 = bf16[2,256,256]{1,2,0:T(8,128)(2,1)S(1)} collective-permute-done((bf16[2,256,256]{1,2,0:T(8,128)(2,1)S(1)}, bf16[2,256,256]{1,2,0:T(8,128)(2,1)S(1)}, u32[]{:S(2)}, u32[]{:S(2)}) %collective-permute-start.5) | collective-permute-done | bytes 262176 | tf_op jit(solution)/shard_map/ppermute | solution.py:35
  180.4 70.6 %custom-call.17 = f32[6,128,128]{2,1,0:T(8,128)S(1)} custom-call(f32[6,128,128]{2,1,0:T(8,128)S(1)} %cholesky.122), custom_call_target="Cholesky" | custom-call | tf_op jit(solution)/shard_map/jit(cholesky)/cholesky | solution.py:99
  252.5 60.4 %custom-call.18 = f32[6,1,128,128]{2,3,1,0:T(8,128)} custom-call(f32[6,1,128,128]{3,2,1,0:T(8,128)} %select_bitcast_fusion), custom_call_target="InvertDiagBlocksLowerTriangular" | custom-call | tf_op jit(solution)/shard_map/jit(cholesky)/cholesky | solution.py:99
  316.1 71.1 %custom-call.19 = f32[6,128,128]{2,1,0:T(8,128)S(1)} custom-call(f32[6,128,128]{2,1,0:T(8,128)} %slice_subtract_fusion), custom_call_target="Cholesky" | custom-call | tf_op jit(solution)/shard_map/jit(cholesky)/cholesky | solution.py:99
  388.8 5.6 %while.1 = (s32[]{:T(128)}, f32[6,256,256]{2,1,0:T(8,128)S(1)}, s32[2,2]{1,0:T(2,128)S(1)}, f32[2,6,128,128]{3,2,0,1:T(8,128)}, s32[]{:T(128)}) while((s32[]{:T(128)}, f32[6,256,256]{2,1,0:T(8,128)S(1)}, s32[2,2]{1,0:T(2,128)S(1)}, f32[2,6,128,128]{3,2,0,1:T(8,128)}, s32[]{:T(128)}) %tuple.44), condition=%wide.while_cond, body=%wide.while_body.sunk | while | flops 2 | bytes 787565 | solution.py:101
  394.4 119.6 %custom-call.20 = f32[6,2,128,128]{2,3,1,0:T(8,128)} custom-call(f32[6,2,128,128]{3,2,1,0:T(8,128)} %bitcast.139), custom_call_target="InvertDiagBlocksLowerTriangular" | custom-call | tf_op jit(solution)/shard_map/vmap(jit(_solve_triangular))/triangular_solve | solution.py:101
  (96 shorter events, 51.2 us)
Async XLA Ops:
  0.6 103.9 %collective-permute-start.1 = (bf16[256,1024]{1,0:T(8,128)(2,1)}, bf16[256,1024]{1,0:T(8,128)(2,1)}, u32[]{:S(2)}, u32[]{:S(2)}) collective-permute-start(bf16[256,1024]{1,0:T(8,128)(2,1)} %param.10), channel_id=1, source_target_pairs={{16,0},{32,16},{48,32},{64,48},{80,64},{96,80},{112,96},{128,112},... | collective-permute-start | bytes 1572872 | tf_op jit(solution)/shard_map/ppermute | solution.py:21
  2.6 102.0 %collective-permute-start = (bf16[256,1024]{1,0:T(8,128)(2,1)}, bf16[256,1024]{1,0:T(8,128)(2,1)}, u32[]{:S(2)}, u32[]{:S(2)}) collective-permute-start(bf16[256,1024]{1,0:T(8,128)(2,1)} %param.10), channel_id=1, source_target_pairs={{0,16},{16,32},{32,48},{48,64},{64,80},{80,96},{96,112},{112,128},... | collective-permute-start | bytes 1572872 | tf_op jit(solution)/shard_map/ppermute | solution.py:20
  6.9 0.7 copy-start.12
  36.9 7.6 %copy-start.8 = (bf16[256,1024]{1,0:T(8,128)(2,1)S(1)}, bf16[256,1024]{1,0:T(8,128)(2,1)}, u32[]{:S(2)}) copy-start(bf16[256,1024]{1,0:T(8,128)(2,1)} %param.11) | copy-start | bytes 1572868
  36.9 90.7 %all-to-all-start = ((bf16[16,2,16384]{2,1,0:T(2,128)(2,1)}), bf16[16,2,16384]{2,1,0:T(2,128)(2,1)}, u32[]{:S(2)}, u32[]{:S(2)}) async-start(bf16[16,2,16384]{2,1,0:T(2,128)(2,1)} %reshape.174), calls=%async_computation | async-start | bytes 2097152 | tf_op jit(solution)/shard_map/all_to_all | solution.py:58
  96.7 7.9 %copy-start.11 = (bf16[256,1024]{1,0:T(8,128)(2,1)S(1)}, bf16[256,1024]{1,0:T(8,128)(2,1)}, u32[]{:S(2)}) copy-start(bf16[256,1024]{1,0:T(8,128)(2,1)} %param.10) | copy-start | bytes 1572868
  97.7 54.9 %collective-permute-start.3 = (bf16[256,1024]{1,0:T(8,128)(2,1)}, bf16[256,1024]{1,0:T(8,128)(2,1)}, u32[]{:S(2)}, u32[]{:S(2)}) collective-permute-start(bf16[256,1024]{1,0:T(8,128)(2,1)} %get-tuple-element.48), channel_id=1, source_target_pairs={{0,16},{16,32},{32,48},{48,64},{64,80},{80,96},{96,112},{112,128},... | collective-permute-start | bytes 1572872 | tf_op jit(solution)/shard_map/ppermute | solution.py:29
  101.8 50.8 %collective-permute-start.2 = (bf16[256,1024]{1,0:T(8,128)(2,1)}, bf16[256,1024]{1,0:T(8,128)(2,1)}, u32[]{:S(2)}, u32[]{:S(2)}) collective-permute-start(bf16[256,1024]{1,0:T(8,128)(2,1)} %get-tuple-element.47), channel_id=1, source_target_pairs={{16,0},{32,16},{48,32},{64,48},{80,64},{96,80},{112,96},{128,112},... | collective-permute-start | bytes 1572872 | tf_op jit(solution)/shard_map/ppermute | solution.py:29
  151.3 1.2 copy-start.5
  152.6 1.8 copy-start
  154.5 4.5 copy-start.2
  156.8 9.2 %collective-permute-start.4 = (bf16[2,256,256]{1,2,0:T(8,128)(2,1)S(1)}, bf16[2,256,256]{1,2,0:T(8,128)(2,1)S(1)}, u32[]{:S(2)}, u32[]{:S(2)}) collective-permute-start(bf16[2,256,256]{1,2,0:T(8,128)(2,1)S(1)} %get-tuple-element.58), channel_id=1, source_target_pairs={{0,1},{1,0},{2,3},{3,2},{4,5},{5,4},{6,7},{7,6},{8,9},{9,8},{10,11... | collective-permute-start | bytes 786440 | tf_op jit(solution)/shard_map/ppermute | solution.py:35
  166.0 9.9 %collective-permute-start.5 = (bf16[2,256,256]{1,2,0:T(8,128)(2,1)S(1)}, bf16[2,256,256]{1,2,0:T(8,128)(2,1)S(1)}, u32[]{:S(2)}, u32[]{:S(2)}) collective-permute-start(bf16[2,256,256]{1,2,0:T(8,128)(2,1)S(1)} %get-tuple-element.37), channel_id=1, source_target_pairs={{0,2},{1,3},{2,0},{3,1},{4,6},{5,7},{6,4},{7,5},{8,10},{9,11},{10,... | collective-permute-start | bytes 786440 | tf_op jit(solution)/shard_map/ppermute | solution.py:35
  176.0 0.8 copy-start.4
  387.6 1.1 copy-start.13
  388.8 125.2 %copy-start.10 = (f32[128,256]{1,0:T(8,128)S(1)}, f32[128,256]{1,0:T(8,128)}, u32[]{:S(2)}) copy-start(f32[128,256]{1,0:T(8,128)} %get-tuple-element.55) | copy-start | bytes 393220
  388.8 127.1 %copy-start.9 = (f32[128,256]{1,0:T(8,128)S(1)}, f32[128,256]{1,0:T(8,128)}, u32[]{:S(2)}) copy-start(f32[128,256]{1,0:T(8,128)} %get-tuple-element.54) | copy-start | bytes 393220
  514.0 2.8 copy-start.7
  515.9 1.7 copy-start.1
  515.9 1.7 copy-start.3
  517.6 2.0 copy-start.6
where the time goes:
time: 535 us; the launch traced here: 524 us
  other arithmetic  336 us (63%)
  local copies, waits for them, and re-layouts  95.4 us (18%)
  matrix products  56.3 us (11%)
  starting transfers between devices  22.7 us (4%)
  waiting for transfers between devices  12.6 us (2%)
    another operation x10, other arithmetic, local(): factors = jnp.linalg.cholesky(stacked_grams)  205 us
    another operation x4, other arithmetic, local(): jax.vmap(partial(jax.scipy.linalg.solve_triangular, lower=True))  122 us
    unnamed x35, local copies, waits for them, and re-layouts  23.5 us
    transpose x1, local copies, waits for them, and re-layouts, local(): jnp.einsum('mda,duai->dumi', conjugate_transpose_rows, stored_sparse_bloc...  22.1 us
    dot_general x1, matrix products, spread_terms(): jnp.einsum('bkg,bksc->sgc', onehot, sketch_products, precision=lax.Precis...  12.8 us
    reshape x1, local copies, waits for them, and re-layouts, local(): (first_child + second_child).astype(jnp.bfloat16)  12.7 us
    all_to_all x1, local copies, waits for them, and re-layouts, local(): lax.all_to_all(extended, 'col', split_axis=2, concat_axis=1, tiled=True)  12.7 us
    ppermute x2, waiting for transfers between devices, from_partner(): return lax.ppermute(value, axis, pairs)  12.5 us
  transfers between devices with their start and end apart: 7, of which 2 were waited for; matrix products, arithmetic and copies ran while one was open for 26% of the time, Pallas kernels for 0%

commit v1 on v0

--- a/solution.py
+++ b/solution.py
@@ -55,7 +55,11 @@
     extended = (
         (first_child + second_child).astype(jnp.bfloat16).reshape(2, samples_here, rows_group)
     )
-    regrouped = lax.all_to_all(extended, "col", split_axis=2, concat_axis=1, tiled=True)
+    view_out = jax.lax.psum(1, "col")
+    part_next = jnp.split(extended, view_out, 2)
+    mid_arr = jnp.stack(part_next, axis=0)
+    high = jax.lax.all_to_all(mid_arr, "col", 0, 0)
+    regrouped = jnp.concatenate(high, 1)
     own_pattern = lax.dynamic_index_in_dim(block_pattern, row_pos, 0, keepdims=False)
     regions = jnp.arange(3 * SLOTS, dtype=jnp.int32) // SLOTS
     flat_index = regions[None, :] * leaf_blocks + own_pattern

time: 535 us -> 500 us (0.935)
  local copies, waits for them, and re-layouts: 95.4 us -> 64.5 us
    reshape x1 -> x0, local copies, waits for them, and re-layouts: 12.7 us -> none  [local(): (first_child + second_child).astype(jnp.bfloat16)]
    all_to_all x1 -> x0, local copies, waits for them, and re-layouts: 12.7 us -> none  [local(): lax.all_to_all(extended, 'col', split_axis=2, concat_axis=1, tiled=True)]
    unnamed x35 -> x46, local copies, waits for them, and re-layouts: 23.5 us -> 13.5 us
  transfers between devices with their start and end apart: 7 -> 7, of which waited for: 2 -> 2; matrix products, arithmetic and copies ran while one was open for 26% -> 21% of each run, Pallas kernels for 0% -> 0%
where the time goes in v1:
time: 500 us; the launch traced here: 491 us
  other arithmetic  334 us (67%)
  local copies, waits for them, and re-layouts  64.5 us (13%)
  matrix products  56.3 us (11%)
  starting transfers between devices  23.8 us (5%)
  waiting for transfers between devices  10.6 us (2%)
    another operation x10, other arithmetic, local(): factors = jnp.linalg.cholesky(stacked_grams)  204 us
    another operation x4, other arithmetic, local(): jax.vmap(partial(jax.scipy.linalg.solve_triangular, lower=True))  122 us
    transpose x1, local copies, waits for them, and re-layouts, local(): jnp.einsum('mda,duai->dumi', conjugate_transpose_rows, stored_sparse_bloc...  22.1 us
    unnamed x46, local copies, waits for them, and re-layouts  13.5 us
    dot_general x1, matrix products, spread_terms(): jnp.einsum('bkg,bksc->sgc', onehot, sketch_products, precision=lax.Precis...  12.8 us
    dot_general x1, matrix products, local(): jnp.einsum('wjht,jhot->wjo', collected_samples, stored_sparse_blocks, pre...  12.4 us
    dot_general x1, matrix products, local(): jnp.einsum('mda,duai->dumi', conjugate_transpose_rows, stored_sparse_bloc...  11.5 us
    ppermute x2, waiting for transfers between devices, from_partner(): return lax.ppermute(value, axis, pairs)  10.6 us
  transfers between devices with their start and end apart: 7, of which 2 were waited for; matrix products, arithmetic and copies ran while one was open for 21% of the time, Pallas kernels for 0%

profile of v1, /device:TPU:98, one launch (start us, length us, event | category | flops | bytes accessed | tf_op | source)
XLA Modules:
  0.0 490.9 jit_solution(12330021450137008400)
XLA Ops:
  2.6 2.4 collective-permute-start
  6.1 11.5 %convolution_bitcast_fusion = f32[8,18,256,128]{2,3,1,0:T(8,128)} fusion(bf16[8,18,128,128]{3,2,1,0:T(8,128)(2,1)} %param.12, bf16[256,8,128,1]{2,1,0,3:T(8,128)(2,1)S(1)} %bitcast.201), kind=kOutput, calls=%fused_computation.7 | convolution fusion | flops 1207959552 | bytes 24117248 | tf_op jit(solution)/shard_map/mda,duai->dumi/dot_general | solution.py:68
  17.6 22.1 %copy.102 = f32[8,18,256,128]{3,1,0,2:T(8,128)} copy(f32[8,18,256,128]{2,3,1,0:T(8,128)} %convolution_bitcast_fusion) | data formatting | bytes 37748736 | tf_op jit(solution)/shard_map/mda,duai->dumi/transpose | solution.py:68
  40.4 12.8 %convolution_bitcast_fusion.1 = f32[256,24,128]{2,1,0:T(8,128)S(1)} fusion(f32[8,18,256,128]{3,1,0,2:T(8,128)} %copy.102, s32[8,18]{1,0:T(8,128)S(1)} %bitcast_add_fusion.1), kind=kOutput, calls=%fused_computation.11 | convolution fusion | flops 1358957952 | bytes 22020672 | tf_op jit(solution)/shard_map/bkg,bksc->sgc/dot_general | solution.py:40
  53.2 2.4 copy.103
  55.6 2.4 copy.104
  59.3 4.6 collective-permute-start.3
  69.8 3.0 gather_fusion.1
  72.8 3.0 gather_fusion
  87.8 8.1 %all-to-all-start = ((bf16[16,2,16,1024]{3,2,1,0:T(8,128)(2,1)}), bf16[16,2,16,1024]{3,2,1,0:T(8,128)(2,1)}, u32[]{:S(2)}, u32[]{:S(2)}) async-start(bf16[16,2,16,1024]{3,2,1,0:T(8,128)(2,1)} %fusion.43), calls=%async_computation | async-start | bytes 2097152 | tf_op jit(solution)/shard_map/all_to_all | solution.py:61
  98.3 6.4 %convert_bitcast_fusion = bf16[256,8,18,128]{3,2,1,0:T(8,128)(2,1)} fusion(bf16[256,24,128,1]{2,1,0,3:T(8,128)(2,1)S(1)} %bitcast.196, s32[8,18]{1,0:T(8,128)S(1)} %bitcast_add_fusion.1), kind=kOutput, calls=%fused_computation.4 | convolution fusion | flops 231214464 | bytes 11010624 | tf_op jit(solution)/shard_map/jhc,wct->wjht/dot_general | solution.py:82
  104.7 12.4 %fusion = f32[8,256,128,1]{1,2,3,0:T(8,128)} fusion(bf16[8,18,128,128]{3,2,1,0:T(8,128)(2,1)} %param.12, bf16[256,8,18,128]{3,2,1,0:T(8,128)(2,1)} %convert_bitcast_fusion), kind=kOutput, calls=%fused_computation.5 | convolution fusion | flops 1207959552 | bytes 15204352 | tf_op jit(solution)/shard_map/wjht,jhot->wjo/dot_general | solution.py:85
  117.0 2.6 copy.99
  123.2 2.3 fusion.75
  127.8 6.0 %collective-permute-done.4 = bf16[2,256,256]{1,2,0:T(8,128)(2,1)S(1)} collective-permute-done((bf16[2,256,256]{1,2,0:T(8,128)(2,1)S(1)}, bf16[2,256,256]{1,2,0:T(8,128)(2,1)S(1)}, u32[]{:S(2)}, u32[]{:S(2)}) %collective-permute-start.4) | collective-permute-done | bytes 262176 | tf_op jit(solution)/shard_map/ppermute | solution.py:35
  133.8 3.2 collective-permute-start.5
  138.3 4.6 collective-permute-done.5
  147.3 70.3 %custom-call.17 = f32[6,128,128]{2,1,0:T(8,128)S(1)} custom-call(f32[6,128,128]{2,1,0:T(8,128)S(1)} %cholesky.122), custom_call_target="Cholesky" | custom-call | tf_op jit(solution)/shard_map/jit(cholesky)/cholesky | solution.py:103
  219.2 60.4 %custom-call.18 = f32[6,1,128,128]{2,3,1,0:T(8,128)} custom-call(f32[6,1,128,128]{3,2,1,0:T(8,128)} %select_bitcast_fusion), custom_call_target="InvertDiagBlocksLowerTriangular" | custom-call | tf_op jit(solution)/shard_map/jit(cholesky)/cholesky | solution.py:103
  282.8 71.1 %custom-call.19 = f32[6,128,128]{2,1,0:T(8,128)S(1)} custom-call(f32[6,128,128]{2,1,0:T(8,128)} %slice_subtract_fusion), custom_call_target="Cholesky" | custom-call | tf_op jit(solution)/shard_map/jit(cholesky)/cholesky | solution.py:103
  355.5 5.6 %while.1 = (s32[]{:T(128)}, f32[6,256,256]{2,1,0:T(8,128)S(1)}, s32[2,2]{1,0:T(2,128)S(1)}, f32[2,6,128,128]{3,2,0,1:T(8,128)}, s32[]{:T(128)}) while((s32[]{:T(128)}, f32[6,256,256]{2,1,0:T(8,128)S(1)}, s32[2,2]{1,0:T(2,128)S(1)}, f32[2,6,128,128]{3,2,0,1:T(8,128)}, s32[]{:T(128)}) %tuple.43), condition=%wide.while_cond, body=%wide.while_body.sunk | while | flops 2 | bytes 787565 | solution.py:105
  356.1 2.2 bitcast_dynamic-update-slice_fusion.2
  358.9 2.2 bitcast_dynamic-update-slice_fusion.2
  361.1 119.5 %custom-call.20 = f32[6,2,128,128]{2,3,1,0:T(8,128)} custom-call(f32[6,2,128,128]{3,2,1,0:T(8,128)} %bitcast.205), custom_call_target="InvertDiagBlocksLowerTriangular" | custom-call | tf_op jit(solution)/shard_map/vmap(jit(_solve_triangular))/triangular_solve | solution.py:105
  (104 shorter events, 54.2 us)
Async XLA Ops:
  0.6 95.9 %collective-permute-start.1 = (bf16[256,1024]{1,0:T(8,128)(2,1)}, bf16[256,1024]{1,0:T(8,128)(2,1)}, u32[]{:S(2)}, u32[]{:S(2)}) collective-permute-start(bf16[256,1024]{1,0:T(8,128)(2,1)} %param.10), channel_id=1, source_target_pairs={{16,0},{32,16},{48,32},{64,48},{80,64},{96,80},{112,96},{128,112},... | collective-permute-start | bytes 1572872 | tf_op jit(solution)/shard_map/ppermute | solution.py:21
  2.6 93.9 %collective-permute-start = (bf16[256,1024]{1,0:T(8,128)(2,1)}, bf16[256,1024]{1,0:T(8,128)(2,1)}, u32[]{:S(2)}, u32[]{:S(2)}) collective-permute-start(bf16[256,1024]{1,0:T(8,128)(2,1)} %param.10), channel_id=1, source_target_pairs={{0,16},{16,32},{32,48},{48,64},{64,80},{80,96},{96,112},{112,128},... | collective-permute-start | bytes 1572872 | tf_op jit(solution)/shard_map/ppermute | solution.py:20
  58.2 7.6 %copy-start.6 = (bf16[2,2,16,16384]{3,2,1,0:T(8,128)(2,1)S(1)}, bf16[2,2,16,16384]{3,2,1,0:T(8,128)(2,1)}, u32[]{:S(2)}) copy-start(bf16[2,2,16,16384]{3,2,1,0:T(8,128)(2,1)} %param.8) | copy-start | bytes 6291460
  59.3 62.0 %collective-permute-start.3 = (bf16[256,1024]{1,0:T(8,128)(2,1)}, bf16[256,1024]{1,0:T(8,128)(2,1)}, u32[]{:S(2)}, u32[]{:S(2)}) collective-permute-start(bf16[256,1024]{1,0:T(8,128)(2,1)} %get-tuple-element.45), channel_id=1, source_target_pairs={{0,16},{16,32},{32,48},{48,64},{64,80},{80,96},{96,112},{112,128},... | collective-permute-start | bytes 1572872 | tf_op jit(solution)/shard_map/ppermute | solution.py:29
  63.9 57.4 %collective-permute-start.2 = (bf16[256,1024]{1,0:T(8,128)(2,1)}, bf16[256,1024]{1,0:T(8,128)(2,1)}, u32[]{:S(2)}, u32[]{:S(2)}) collective-permute-start(bf16[256,1024]{1,0:T(8,128)(2,1)} %get-tuple-element.44), channel_id=1, source_target_pairs={{16,0},{32,16},{48,32},{64,48},{80,64},{96,80},{112,96},{128,112},... | collective-permute-start | bytes 1572872 | tf_op jit(solution)/shard_map/ppermute | solution.py:29
  66.2 1.7 copy-start.11
  87.8 31.8 %all-to-all-start = ((bf16[16,2,16,1024]{3,2,1,0:T(8,128)(2,1)}), bf16[16,2,16,1024]{3,2,1,0:T(8,128)(2,1)}, u32[]{:S(2)}, u32[]{:S(2)}) async-start(bf16[16,2,16,1024]{3,2,1,0:T(8,128)(2,1)} %fusion.43), calls=%async_computation | async-start | bytes 2097152 | tf_op jit(solution)/shard_map/all_to_all | solution.py:61
  119.6 1.5 copy-start.5
  121.3 1.9 copy-start.2
  123.2 4.6 copy-start
  125.5 8.2 %collective-permute-start.4 = (bf16[2,256,256]{1,2,0:T(8,128)(2,1)S(1)}, bf16[2,256,256]{1,2,0:T(8,128)(2,1)S(1)}, u32[]{:S(2)}, u32[]{:S(2)}) collective-permute-start(bf16[2,256,256]{1,2,0:T(8,128)(2,1)S(1)} %get-tuple-element.55), channel_id=1, source_target_pairs={{0,1},{1,0},{2,3},{3,2},{4,5},{5,4},{6,7},{7,6},{8,9},{9,8},{10,11... | collective-permute-start | bytes 786440 | tf_op jit(solution)/shard_map/ppermute | solution.py:35
  133.8 9.1 %collective-permute-start.5 = (bf16[2,256,256]{1,2,0:T(8,128)(2,1)S(1)}, bf16[2,256,256]{1,2,0:T(8,128)(2,1)S(1)}, u32[]{:S(2)}, u32[]{:S(2)}) collective-permute-start(bf16[2,256,256]{1,2,0:T(8,128)(2,1)S(1)} %get-tuple-element.34), channel_id=1, source_target_pairs={{0,2},{1,3},{2,0},{3,1},{4,6},{5,7},{6,4},{7,5},{8,10},{9,11},{10,... | collective-permute-start | bytes 786440 | tf_op jit(solution)/shard_map/ppermute | solution.py:35
  142.9 0.8 copy-start.4
  354.3 1.1 copy-start.12
  355.5 125.2 %copy-start.10 = (f32[128,256]{1,0:T(8,128)S(1)}, f32[128,256]{1,0:T(8,128)}, u32[]{:S(2)}) copy-start(f32[128,256]{1,0:T(8,128)} %get-tuple-element.52) | copy-start | bytes 393220
  355.5 127.1 %copy-start.9 = (f32[128,256]{1,0:T(8,128)S(1)}, f32[128,256]{1,0:T(8,128)}, u32[]{:S(2)}) copy-start(f32[128,256]{1,0:T(8,128)} %get-tuple-element.51) | copy-start | bytes 393220
  480.7 2.8 copy-start.8
  482.6 1.7 copy-start.1
  482.6 1.7 copy-start.3
  484.3 2.0 copy-start.7
